TPU v7x, 32 devices: a whole 2x2x4 slice. The times are simulated.
32 devices in a mesh: dp: 4 (over x, core), expert: 8 (over z, y).
Axes of the slice: x: 2, y: 2, z: 4, core: 2. Of those that a mesh axis runs over, the one named last changes fastest.
Arguments:
- tokens: bfloat16 [6144, 1024], P(('dp', 'expert')), may hold values from -6 to 6
- route_ids: int32 [6144, 4], P(('dp', 'expert')), may hold values from 0 to 7, all different within a row; in each aligned block of 192 rows (0 to 191, 192 to 383, ...) at most 144 rows name the same one
- gate_weight: float32 [6144, 4], P(('dp', 'expert')), may hold values from 0.25 to 1
- old_owner: int32 [8], replicated, may hold values from 0 to 7, as said below
- new_owner: int32 [8], replicated, may hold values from 0 to 7, as said below
- weights: bfloat16 [8, 3, 1024, 1024], P('expert', None, None, 'dp'), may hold values from -0.1875 to 0.1875
- first_moment: float32 [8, 3, 1024, 1024], P('expert', None, None, 'dp'), may hold values from -6 to 6
- second_moment: float32 [8, 3, 1024, 1024], P('expert', None, None, 'dp'), may hold values from 0.01 to 4
Outputs:
- layer_output: bfloat16 [6144, 1024], P(('dp', 'expert'))
- new_weights: bfloat16 [8, 3, 1024, 1024], P('expert', None, None, 'dp')
- new_first_moment: float32 [8, 3, 1024, 1024], P('expert', None, None, 'dp')
- new_second_moment: float32 [8, 3, 1024, 1024], P('expert', None, None, 'dp')
Inputs may be any that keep to these rules, and one draw needn't show every extreme that they name: `old_owner`: A permutation of the slots. `new_owner`: A permutation of the slots that differs from old_owner in exactly 2 experts. `route_ids`: the 4 experts of a row differ. In the 192 rows of one device no expert is named more than 144 times, a bound that some block reaches.
All inputs are finite; a program needn't handle non-finite values.
Results may differ from a plain program's by a relative error of at most 0.0058.
Values may be sent and summed in bfloat16 or wider, within the bound.
No kernel may reach another device: no remote copies, remote signals or barrier semaphores. Data moves between devices by JAX's collectives and lax.ppermute only.
A program may use at most 128 MiB of HBM per device.

v0:
```python
import functools
import itertools

import jax
import jax.numpy as jnp
from jax import lax
from jax.experimental import pallas as pl
from jax.experimental.pallas import tpu as pltpu
from jax.sharding import PartitionSpec as P


LANES = 128
PAIR_LIMIT = 64
EXPERT_VMEM = 16 << 20
MOVE_VMEM = 16 << 20


def ring_pairs(count):
    order = list(range(0, count, 2)) + list(range(1, count, 2))[::-1]
    ahead = [(order[i], order[(i + 1) % count]) for i in range(count)]
    return ahead, [(b, a) for a, b in ahead]


def relay_of(source, target, count):
    if source ^ 1 != target:
        return source ^ 1
    beyond = target + 2
    return beyond if beyond < count else target - 2


def swap_slots(pair, dp_count, count, weights, moments):
    low, high = pair
    low_relay, high_relay = relay_of(low, high, count), relay_of(high, low, count)

    def spread(core, edges):
        return [
            (row * count + a, row * count + b) for row in range(core, dp_count, 2) for a, b in edges
        ]

    swap = [(low, high), (high, low)]
    first_hop = spread(1, [(low, low_relay), (high, high_relay)])
    second_hop = spread(1, [(low_relay, high), (high_relay, low)])
    axes = ("dp", "expert")
    direct = lax.ppermute(moments, axes, spread(0, swap) + first_hop)
    moved_weights = lax.ppermute(weights, axes, spread(0, swap) + spread(1, swap))
    relayed = lax.ppermute(direct, axes, second_hop)
    return moved_weights, direct, relayed


def any_permutation(source_slot, weights, moments):
    count, lanes = lax.axis_size("expert"), weights.shape[-1]
    rows = jnp.concatenate([b.reshape(count, -1, lanes) for b in (weights, moments)], axis=1)
    spread = lax.all_to_all(rows, "expert", split_axis=0, concat_axis=0, tiled=True)
    ordered = jnp.take(spread, source_slot, axis=0)
    back = lax.all_to_all(ordered, "expert", split_axis=0, concat_axis=0, tiled=True)
    cut = weights.size // (count * lanes)
    moved = back[:, cut:].reshape(moments.shape)
    return back[:, :cut].reshape(weights.shape), moved, moved


def pack_kernel(first_ref, second_ref, out_ref):
    out_ref[0] = first_ref[0].astype(jnp.bfloat16)
    out_ref[1] = second_ref[0].astype(jnp.bfloat16)


def pack_moments(first_moment, second_moment):
    _, parts, rows, lanes = first_moment.shape
    block = (1, 1, rows, lanes)
    return pl.pallas_call(
        pack_kernel,
        grid=(parts,),
        out_shape=jax.ShapeDtypeStruct((2, parts, rows, lanes), jnp.bfloat16),
        in_specs=[pl.BlockSpec(block, lambda i: (0, i, 0, 0))] * 2,
        out_specs=pl.BlockSpec((2, 1, rows, lanes), lambda i: (0, i, 0, 0)),
        cost_estimate=pl.CostEstimate(
            flops=first_moment.size, bytes_accessed=12 * first_moment.size, transcendentals=0
        ),
    )(first_moment, second_moment)


def unpack_kernel(parts, flags, *refs):
    weights, first, second, arrived, direct, relayed = refs[:6]
    out_weights, out_first, out_second = refs[6:9]
    held, wide, narrow, reads, writes = refs[9:]
    here, odd = flags[0] == 1, flags[1] == 1
    owns, outs = (first, second), (out_first, out_second)
    pieces = [(k, i) for k in range(2) for i in range(parts)]
    last = len(pieces)

    def own_read(n):
        k, i = pieces[n]
        return pltpu.make_async_copy(owns[k].at[0, i], wide.at[n], reads.at[n])

    def moved_read(n, source):
        k, i = pieces[n]
        return pltpu.make_async_copy(source.at[k, i], narrow.at[n], reads.at[n])

    def write(n):
        k, i = pieces[n]
        return pltpu.make_async_copy(wide.at[n], outs[k].at[0, i], writes.at[n])

    to_held = pltpu.make_async_copy(weights, held, reads.at[last])
    to_held_moved = pltpu.make_async_copy(arrived, held, reads.at[last])
    from_held = pltpu.make_async_copy(held, out_weights, writes.at[last])

    @pl.when(jnp.logical_not(here))
    def _():
        for n in range(last):
            own_read(n).start()
        to_held.start()
        for n in range(last):
            own_read(n).wait()
            write(n).start()
        to_held.wait()

    @pl.when(here)
    def _():
        @pl.when(odd)
        def _():
            for n in range(last):
                moved_read(n, relayed).start()

        @pl.when(jnp.logical_not(odd))
        def _():
            for n in range(last):
                moved_read(n, direct).start()

        to_held_moved.start()
        for n in range(last):
            moved_read(n, direct).wait()
            wide[n] = narrow[n].astype(jnp.float32)
            write(n).start()
        to_held_moved.wait()

    from_held.start()
    for n in range(last):
        write(n).wait()
    from_held.wait()


def unpack(flags, weights, first, second, arrived, direct, relayed):
    _, parts, rows, lanes = weights.shape
    anywhere = pl.BlockSpec(memory_space=pl.ANY)
    return pl.pallas_call(
        functools.partial(unpack_kernel, parts),
        out_shape=[jax.ShapeDtypeStruct(a.shape, a.dtype) for a in (weights, first, second)],
        in_specs=[pl.BlockSpec(memory_space=pltpu.SMEM)] + [anywhere] * 6,
        out_specs=[anywhere] * 3,
        scratch_shapes=[
            pltpu.VMEM(weights.shape, weights.dtype),
            pltpu.VMEM((2 * parts, rows, lanes), jnp.float32),
            pltpu.VMEM((2 * parts, rows, lanes), jnp.bfloat16),
            pltpu.SemaphoreType.DMA((2 * parts + 1,)),
            pltpu.SemaphoreType.DMA((2 * parts + 1,)),
        ],
        compiler_params=pltpu.CompilerParams(vmem_limit_bytes=MOVE_VMEM),
        cost_estimate=pl.CostEstimate(
            flops=weights.size, bytes_accessed=20 * weights.size, transcendentals=0
        ),
    )(flags, weights, first, second, arrived, direct, relayed)


def relocate(weights, packed, others, meanwhile, old_owner, new_owner, source_slot, dp_count, count):
    pairs = list(itertools.combinations(range(count), 2))
    if len(pairs) > PAIR_LIMIT:
        return any_permutation(source_slot, weights, packed), meanwhile(weights, *others)
    pairs.sort(key=lambda pair: pair[::-1])
    differs = old_owner != new_owner
    low = jnp.min(jnp.where(differs, old_owner, count))
    high = jnp.max(jnp.where(differs, old_owner, 0))
    number = lax.shift_right_logical(high * (high - 1), 1) + low
    branch = jnp.where(jnp.sum(differs.astype(jnp.int32)) == 2, number, len(pairs))

    def moving(pair, weights, packed, others):
        moved = swap_slots(pair, dp_count, count, weights, packed)
        return moved, meanwhile(weights, *others)

    def moving_any(weights, packed, others):
        return any_permutation(source_slot, weights, packed), meanwhile(weights, *others)

    branches = [functools.partial(moving, pair) for pair in pairs] + [moving_any]
    return lax.switch(branch, branches, weights, packed, others)


def expert_kernel(blocks, shards, tok_rows, slot_ref, *refs):
    rows_refs, far_refs, out_refs = (
        refs[:blocks],
        refs[blocks : blocks + shards],
        refs[blocks + shards : -3],
    )
    held, total, arrivals = refs[-3:]

    def fetch(i, source):
        return pltpu.make_async_copy(source.at[0], held.at[i], arrivals.at[i])

    for i, ref in enumerate(far_refs):
        fetch(i, ref).start()
    rows = jnp.concatenate([r[:tok_rows] for r in rows_refs], axis=0)
    slot = slot_ref[0]
    offset = -(-tok_rows // LANES) * LANES
    gates = []
    for r in rows_refs:
        table = r[tok_rows:].astype(jnp.float32)
        column = (table[:, :offset] + table[:, offset : 2 * offset]).T
        mine = lax.broadcasted_iota(jnp.int32, column.shape, 1) == slot
        column = jnp.sum(jnp.where(mine, column, 0.0), axis=1, keepdims=True)
        gates.append(column[:tok_rows])
    gate = jnp.concatenate(gates, axis=0)
    total[...] = jnp.zeros_like(total)

    @pl.loop(0, shards)
    def _(i):
        fetch(i, far_refs[0]).wait()
        g = jnp.dot(rows, held[i, 0], preferred_element_type=jnp.float32)
        u = jnp.dot(rows, held[i, 1], preferred_element_type=jnp.float32)
        hidden = (g / (1.0 + jnp.exp(-g)) * u).astype(jnp.bfloat16)
        total[...] += lax.dot_general(
            hidden, held[i, 2], (((1,), (1,)), ((), ())), preferred_element_type=jnp.float32
        )

    result = total[...].astype(jnp.bfloat16).astype(jnp.float32) * gate
    start = 0
    for out in out_refs:
        out[...] = result[start : start + out.shape[0]].astype(out.dtype)
        start += out.shape[0]


def run_expert(slot, row_blocks, dtype, pieces, shards, tok_rows):
    blocks = len(row_blocks)
    whole = pl.BlockSpec(memory_space=pltpu.VMEM)
    _, _, width, hidden = shards[0].shape
    rows, hidden = blocks * tok_rows, hidden * len(shards)
    piece = jax.ShapeDtypeStruct((tok_rows // pieces, width), dtype)
    return pl.pallas_call(
        functools.partial(expert_kernel, blocks, len(shards), tok_rows),
        out_shape=[piece] * (pieces * blocks),
        in_specs=[pl.BlockSpec(memory_space=pltpu.SMEM)]
        + [whole] * blocks
        + [pl.BlockSpec(memory_space=pl.ANY)] * len(shards),
        out_specs=[whole] * (pieces * blocks),
        scratch_shapes=[
            pltpu.VMEM((len(shards),) + shards[0].shape[1:], shards[0].dtype),
            pltpu.VMEM((rows, width), jnp.float32),
            pltpu.SemaphoreType.DMA((len(shards),)),
        ],
        compiler_params=pltpu.CompilerParams(vmem_limit_bytes=EXPERT_VMEM),
        cost_estimate=pl.CostEstimate(
            flops=6 * rows * width * hidden,
            bytes_accessed=6 * width * hidden + 6 * rows * width,
            transcendentals=rows * hidden,
        ),
    )(slot, *row_blocks, *shards)


def whole(
    tokens, route_ids, gate_weight, old_owner, new_owner, weights, first_moment, second_moment
):
    count, dp_count = lax.axis_size("expert"), lax.axis_size("dp")
    tok_rows, width = tokens.shape
    odd = lax.bitwise_and(lax.axis_index("dp"), 1) == 1
    labels = jnp.arange(count, dtype=jnp.int32)
    source_slot = jnp.sum(
        jnp.where(new_owner[None, :] == labels[:, None], old_owner[None, :], 0), axis=1
    )
    slot = lax.axis_index("expert").astype(jnp.int32)

    by_expert = jnp.sum(
        jnp.where(route_ids[:, :, None] == labels[None, None, :], gate_weight[:, :, None], 0.0),
        axis=1,
    )
    by_slot = jnp.sum(
        jnp.where(old_owner[None, None, :] == labels[:, None, None], by_expert[None, :, :], 0.0),
        axis=2,
    )
    high = by_slot.astype(jnp.bfloat16)
    low = (by_slot - high.astype(jnp.float32)).astype(jnp.bfloat16)
    offset = -(-tok_rows // LANES) * LANES
    spare = -count % 8
    high = jnp.pad(high, ((0, spare), (0, offset - tok_rows)))
    low = jnp.pad(low, ((0, spare), (0, width - offset - tok_rows)))
    packed = jnp.concatenate([tokens, jnp.concatenate([high, low], axis=1)], axis=0)

    ahead, behind = ring_pairs(count)
    opposite = [
        (row * count + a, row * count + b)
        for row in range(dp_count)
        for a, b in (behind if row % 2 else ahead)
    ]
    swap = [(i, i ^ 1) for i in range(dp_count)]
    steps = count // 2

    def hop(back, front):
        return lax.ppermute(back, "expert", ahead), lax.ppermute(front, "expert", behind)

    def run(shards, blocks, dtype=jnp.float32, pieces=2):
        return list(run_expert(slot.reshape(1), blocks, dtype, pieces, shards, tok_rows))

    hops = {1: hop(packed, packed)}
    moments = pack_moments(first_moment, second_moment)

    def meanwhile(weights, back, front):
        second = hop(back, front) if steps > 2 else ()
        shards = [weights, lax.ppermute(weights, "dp", swap)]
        for step in range(1, dp_count // 2):
            turn = [(i, (i + 2 * step) % dp_count) for i in range(dp_count)]
            far = lax.ppermute(weights, "dp", turn)
            far, shards[-1] = lax.optimization_barrier((far, shards[-1]))
            shards += [far, lax.ppermute(far, "dp", swap)]
        return second, shards[1:]

    moved, (second, shards) = relocate(
        weights,
        moments,
        hops[1],
        meanwhile,
        old_owner,
        new_owner,
        source_slot,
        dp_count,
        count,
    )
    moved = lax.optimization_barrier(moved)
    shards = [weights, *shards]
    if second:
        hops[2] = second
    for step in range(3, steps):
        hops[step] = hop(*hops[step - 1])
    answers = {1: run(shards, [packed, *hops[1]])}
    own, answers[1] = answers[1][:2], answers[1][2:]
    for step in range(2, steps):
        answers[step] = run(shards, list(hops[step]))
    farthest = lax.ppermute(
        jnp.where(odd, *hops[steps - 1][::-1]), ("dp", "expert"), opposite
    )
    (outermost,) = run(shards, [farthest], jnp.bfloat16, 1)
    arrived = lax.ppermute(outermost, ("dp", "expert"), opposite).astype(jnp.float32)

    outputs = []
    for half in range(2):
        part = arrived[half * tok_rows // 2 : (half + 1) * tok_rows // 2]
        to_behind, to_ahead = jnp.where(odd, part, 0.0), jnp.where(odd, 0.0, part)
        for step in range(steps - 1, 0, -1):
            back = (answers[step][half] + to_behind).astype(jnp.bfloat16)
            front = (answers[step][2 + half] + to_ahead).astype(jnp.bfloat16)
            to_behind = lax.ppermute(back, "expert", behind).astype(jnp.float32)
            to_ahead = lax.ppermute(front, "expert", ahead).astype(jnp.float32)
        outputs.append((own[half] + to_behind + to_ahead).astype(jnp.bfloat16))
    layer_output = jnp.concatenate(outputs, axis=0)

    here = jnp.sum(jnp.where(labels == slot, source_slot, 0)) != slot
    flags = jnp.stack([here, odd]).astype(jnp.int32)
    replaced = unpack(flags, weights, first_moment, second_moment, *moved)
    return (layer_output, *replaced)


def solution(mesh):
    placed = (
        P(("dp", "expert"), None),
        P(("dp", "expert"), None),
        P(("dp", "expert"), None),
        P(),
        P(),
        P("expert", None, None, "dp"),
        P("expert", None, None, "dp"),
        P("expert", None, None, "dp"),
    )
    return jax.shard_map(
        whole,
        mesh=mesh,
        in_specs=placed,
        out_specs=(
            P(("dp", "expert"), None),
            P("expert", None, None, "dp"),
            P("expert", None, None, "dp"),
            P("expert", None, None, "dp"),
        ),
        check_vma=False,
    )
```

profile of v0, /device:TPU:1, one launch (start us, length us, event | category | flops | bytes accessed | tf_op | source)
XLA Modules:
  0.0 184.4 jit_solution(16407544825326905669)
XLA Ops:
  0.6 0.7 iota_compare_fusion.5
  1.3 0.7 select_reduce_fusion.1
  2.0 0.1 select_reduce_fusion
  2.1 1.0 fusion.7.refs_0_
  3.2 2.2 %collective-permute-start.229 = (bf16[200,1024]{1,0:T(8,128)(2,1)S(1)}, bf16[200,1024]{1,0:T(8,128)(2,1)}, u32[]{:S(2)}, u32[]{:S(2)}) collective-permute-start(bf16[200,1024]{1,0:T(8,128)(2,1)S(1)} %fusion.7.refs_0_), channel_id=1, source_target_pairs={{0,2},{2,4},{4,6},{6,7},{7,5},{5,3},{3,1},{1,0},{8,10},{10,12},{12... | collective-permute-start | bytes 1228808 | tf_op jit(solution)/shard_map/ppermute | solution.py:293
  5.3 0.0 collective-permute-start.230
  5.3 1.3 select_reduce_fusion.3
  9.3 0.0 copy-start.4
  9.3 5.3 %shard_map.111 = bf16[2,3,1024,256]{3,2,1,0:T(8,128)(2,1)} custom-call(f32[1,3,1024,256]{3,2,1,0:T(8,128)} %refs_1_.3, f32[1,3,1024,256]{3,2,1,0:T(8,128)} %refs_2_.5), custom_call_target="tpu_custom_call" | custom-call | flops 786432 | bytes 9437184 | tf_op jit(solution)/shard_map/pallas_call | solution.py:69
  14.6 0.1 select_reduce_fusion.2
  14.7 0.8 collective-permute-done.230.refs_2_
  15.5 90.6 %conditional.1 = (bf16[1,3,1024,256]{3,2,1,0:T(8,128)(2,1)}, bf16[2,3,1024,256]{3,2,1,0:T(8,128)(2,1)}, bf16[2,3,1024,256]{3,2,1,0:T(8,128)(2,1)}, bf16[200,1024...) conditional(s32[]{:T(128)} %clamp.3, ...), branch_computations={%region_6.7_spmd, %region_7.8_spmd, %region_8.9_spmd, %region_9.10... | conditional | flops 11797576 | bytes 94507512 | solution.py:182
  15.5 6.9 %collective-permute-start.33 = (bf16[2,3,1024,256]{3,2,1,0:T(8,128)(2,1)}, bf16[2,3,1024,256]{3,2,1,0:T(8,128)(2,1)}, u32[]{:S(2)}, u32[]{:S(2)}) collective-permute-start(bf16[2,3,1024,256]{3,2,1,0:T(8,128)(2,1)} %get-tuple-element.259), channel_id=1, source_target_pairs={{1,3},{3,1},{17,19},{19,17},{9,8},{11,10},{25,24},{27,26}} | collective-permute-start | bytes 9437192 | tf_op jit(solution)/shard_map/cond/branch_4_fun/ppermute | solution.py:44
  22.4 1.4 collective-permute-start.37
  23.8 2.3 %collective-permute-start.38 = (bf16[1,3,1024,256]{3,2,1,0:T(8,128)(2,1)S(1)}, bf16[1,3,1024,256]{3,2,1,0:T(8,128)(2,1)}, u32[]{:S(2)}, u32[]{:S(2)}) collective-permute-start(bf16[1,3,1024,256]{3,2,1,0:T(8,128)(2,1)S(1)} %get-tuple-element.258), channel_id=1, source_target_pairs={{0,8},{8,0},{16,24},{24,16},{1,9},{9,1},{17,25},{25,17},{2,10},{10... | collective-permute-start | bytes 4718600 | tf_op jit(solution)/shard_map/cond/branch_4_fun/ppermute | solution.py:303
  26.1 33.3 %collective-permute-done.33 = bf16[2,3,1024,256]{3,2,1,0:T(8,128)(2,1)} collective-permute-done((bf16[2,3,1024,256]{3,2,1,0:T(8,128)(2,1)}, bf16[2,3,1024,256]{3,2,1,0:T(8,128)(2,1)}, u32[]{:S(2)}, u32[]{:S(2)}) %collective-permute-start.33) | collective-permute-done | bytes 3145760 | tf_op jit(solution)/shard_map/cond/branch_4_fun/ppermute | solution.py:44
  59.4 4.1 %collective-permute-start.34 = (bf16[2,3,1024,256]{3,2,1,0:T(8,128)(2,1)}, bf16[2,3,1024,256]{3,2,1,0:T(8,128)(2,1)}, u32[]{:S(2)}, u32[]{:S(2)}) collective-permute-start(bf16[2,3,1024,256]{3,2,1,0:T(8,128)(2,1)} %collective-permute-done.33), channel_id=1, source_target_pairs={{8,11},{10,9},{24,27},{26,25}} | collective-permute-start | bytes 9437192 | tf_op jit(solution)/shard_map/cond/branch_4_fun/ppermute | solution.py:46
  63.4 3.7 %collective-permute-start.32 = (bf16[1,3,1024,256]{3,2,1,0:T(8,128)(2,1)S(1)}, bf16[1,3,1024,256]{3,2,1,0:T(8,128)(2,1)}, u32[]{:S(2)}, u32[]{:S(2)}) collective-permute-start(bf16[1,3,1024,256]{3,2,1,0:T(8,128)(2,1)S(1)} %get-tuple-element.258), channel_id=1, source_target_pairs={{1,3},{3,1},{17,19},{19,17},{9,11},{11,9},{25,27},{27,25}} | collective-permute-start | bytes 4718600 | tf_op jit(solution)/shard_map/cond/branch_4_fun/ppermute | solution.py:45
  67.1 0.1 collective-permute-start.39
  67.3 1.6 collective-permute-start.35
  68.9 36.1 %collective-permute-done.35 = bf16[200,1024]{1,0:T(8,128)(2,1)} collective-permute-done((bf16[200,1024]{1,0:T(8,128)(2,1)}, bf16[200,1024]{1,0:T(8,128)(2,1)}, u32[]{:S(2)}, u32[]{:S(2)}) %collective-permute-start.35) | collective-permute-done | bytes 409632 | tf_op jit(solution)/shard_map/cond/branch_4_fun/ppermute | solution.py:293
  105.0 0.8 collective-permute-done.36
  106.1 1.2 collective-permute-start.231
  107.3 5.5 %collective-permute-start.232 = (bf16[200,1024]{1,0:T(8,128)(2,1)}, bf16[200,1024]{1,0:T(8,128)(2,1)S(1)}, u32[]{:S(2)}, u32[]{:S(2)}) collective-permute-start(bf16[200,1024]{1,0:T(8,128)(2,1)} %get-tuple-element.447.refs_1_), channel_id=1, source_target_pairs={{2,0},{4,2},{6,4},{7,6},{5,7},{3,5},{1,3},{0,1},{10,8},{12,10},{14... | collective-permute-start | bytes 1228808 | tf_op jit(solution)/shard_map/ppermute | solution.py:293
  112.8 9.0 %collective-permute-done.231.refs_0_ = bf16[200,1024]{1,0:T(8,128)(2,1)S(1)} collective-permute-done((bf16[200,1024]{1,0:T(8,128)(2,1)}, bf16[200,1024]{1,0:T(8,128)(2,1)S(1)}, u32[]{:S(2)}, u32[]{:S(2)}) %collective-permute-start.231) | collective-permute-done | bytes 409632 | tf_op jit(solution)/shard_map/ppermute | solution.py:293
  121.8 0.8 broadcast_select_fusion.1
  122.6 1.2 collective-permute-start.233
  123.9 0.6 fusion.8
  125.2 0.1 add_convert_fusion.14.flags
  125.2 4.7 %collective-permute-done.233.refs_0_ = bf16[200,1024]{1,0:T(8,128)(2,1)S(1)} collective-permute-done((bf16[200,1024]{1,0:T(8,128)(2,1)}, bf16[200,1024]{1,0:T(8,128)(2,1)S(1)}, u32[]{:S(2)}, u32[]{:S(2)}) %collective-permute-start.233) | collective-permute-done | bytes 409632 | tf_op jit(solution)/shard_map/ppermute | solution.py:332
  129.9 3.5 %shard_map.115 = bf16[192,1024]{1,0:T(8,128)(2,1)S(1)} custom-call(s32[1]{0:T(128)} %bitcast.4.slot_ref, bf16[200,1024]{1,0:T(8,128)(2,1)S(1)} %collective-permute-done.233.refs_0_, bf16[1,3,1024,256]{3,2,1,0:T(8,128)(2,1)S(1)} %copy-done.2, bf16[1,3,1024,256]{3,2,1,0:T(8,128)(2,1)} %get-tuple-element.441.refs_4_.refs_3_.refs_2_, ...), custom_call_target="tpu_custom_call" | custom-call | flops 1207959552 | bytes 7471104 | tf_op jit(solution)/shard_map/pallas_call | solution.py:234
  133.5 1.3 collective-permute-start.234
  134.8 7.1 %shard_map.112 = (f32[96,1024]{1,0:T(8,128)S(1)}, f32[96,1024]{1,0:T(8,128)S(1)}, f32[96,1024]{1,0:T(8,128)S(1)}, f32[96,1024]{1,0:T(8,128)S(1)}, f32[96,1024]{1,0:T(8,128)S(1)}, /*index=5*/f32[96,1024]{1,0:T(8,128)S(1)}) custom-call(s32[1]{0:T(128)} %bitcast.4.slot_ref, bf16[200,1024]{1,0:T(8,128)(2,1)S(1)} %fusion.7.refs_0_, ...), custom_call_target="tpu_custom_call" | custom-call | flops 3623878656 | bytes 9830400 | tf_op jit(solution)/shard_map/pallas_call | solution.py:234
  141.9 4.4 %shard_map.116 = (bf16[1,3,1024,256]{3,2,1,0:T(8,128)(2,1)}, f32[1,3,1024,256]{3,2,1,0:T(8,128)}, f32[1,3,1024,256]{3,2,1,0:T(8,128)}) custom-call(s32[2]{0:T(128)S(1)} %add_convert_fusion.14.flags, bf16[1,3,1024,256]{3,2,1,0:T(8,128)(2,1)S(1)} %copy-done.2, f32[1,3,1024,256]{3,2,1,0:T(8,128)S(1)} %copy-done, f32[1,3,1024,256]{3,2,1,0:T(8,128)S(1)} %copy-done.1, ...), custom_call_target="tpu_custom_call" | custom-call | flops 786432 | bytes 15728640 | tf_op jit(solution)/shard_map/pallas_call | solution.py:144
  146.2 4.3 %shard_map.114 = (f32[96,1024]{1,0:T(8,128)S(1)}, f32[96,1024]{1,0:T(8,128)S(1)}, f32[96,1024]{1,0:T(8,128)S(1)}, f32[96,1024]{1,0:T(8,128)S(1)}) custom-call(s32[1]{0:T(128)} %bitcast.4.slot_ref, bf16[200,1024]{1,0:T(8,128)(2,1)S(1)} %collective-permute-done.231.refs_0_, bf16[200,1024]{1,0:T(8,128)(2,1)S(1)} %collective-permute-done.232.refs_1_, ...), custom_call_target="tpu_custom_call" | custom-call | flops 2415919104 | bytes 8650752 | tf_op jit(solution)/shard_map/pallas_call | solution.py:234
  150.5 0.1 convert_element_type.104
  150.6 0.3 add_convert_fusion.13
  150.9 1.8 collective-permute-start.235
  152.6 5.4 %shard_map.113 = (f32[96,1024]{1,0:T(8,128)S(1)}, f32[96,1024]{1,0:T(8,128)S(1)}, f32[96,1024]{1,0:T(8,128)S(1)}, f32[96,1024]{1,0:T(8,128)S(1)}) custom-call(s32[1]{0:T(128)} %bitcast.4.slot_ref, bf16[200,1024]{1,0:T(8,128)(2,1)} %get-tuple-element.446.refs_0_, bf16[200,1024]{1,0:T(8,128)(2,1)} %get-tuple-element.447.refs_1_, ...), custom_call_target="tpu_custom_call" | custom-call | flops 2415919104 | bytes 8650752 | tf_op jit(solution)/shard_map/pallas_call | solution.py:234
  158.0 0.1 collective-permute-start.238
  158.1 1.5 collective-permute-start.241
  159.6 0.1 collective-permute-start.244
  159.7 1.5 collective-permute-start.236
  161.1 1.5 collective-permute-done.238
  162.6 0.1 add_convert_fusion.9
  162.7 0.4 collective-permute-start.239
  163.1 1.2 collective-permute-start.242
  164.3 2.4 %collective-permute-done.244 = bf16[96,1024]{1,0:T(8,128)(2,1)S(1)} collective-permute-done((bf16[96,1024]{1,0:T(8,128)(2,1)S(1)}, bf16[96,1024]{1,0:T(8,128)(2,1)S(1)}, u32[]{:S(2)}, u32[]{:S(2)}) %collective-permute-start.244) | collective-permute-done | bytes 196640 | tf_op jit(solution)/shard_map/ppermute | solution.py:346
  166.7 0.3 collective-permute-start.245
  167.1 0.1 add_convert_fusion.11
  167.1 1.2 collective-permute-start.237
  168.4 2.5 %collective-permute-done.239 = bf16[96,1024]{1,0:T(8,128)(2,1)S(1)} collective-permute-done((bf16[96,1024]{1,0:T(8,128)(2,1)S(1)}, bf16[96,1024]{1,0:T(8,128)(2,1)S(1)}, u32[]{:S(2)}, u32[]{:S(2)}) %collective-permute-start.239) | collective-permute-done | bytes 196640 | tf_op jit(solution)/shard_map/ppermute | solution.py:346
  170.9 0.1 add_convert_fusion.8
  171.0 0.3 collective-permute-start.240
  171.3 0.1 add_convert_fusion.4
  171.4 1.2 collective-permute-start.243
  172.6 2.5 %collective-permute-done.245 = bf16[96,1024]{1,0:T(8,128)(2,1)S(1)} collective-permute-done((bf16[96,1024]{1,0:T(8,128)(2,1)S(1)}, bf16[96,1024]{1,0:T(8,128)(2,1)S(1)}, u32[]{:S(2)}, u32[]{:S(2)}) %collective-permute-start.245) | collective-permute-done | bytes 196640 | tf_op jit(solution)/shard_map/ppermute | solution.py:346
  175.1 0.1 add_convert_fusion.1
  175.2 0.3 collective-permute-start.246
  175.5 3.8 %collective-permute-done.240 = bf16[96,1024]{1,0:T(8,128)(2,1)S(1)} collective-permute-done((bf16[96,1024]{1,0:T(8,128)(2,1)S(1)}, bf16[96,1024]{1,0:T(8,128)(2,1)S(1)}, u32[]{:S(2)}, u32[]{:S(2)}) %collective-permute-start.240) | collective-permute-done | bytes 196640 | tf_op jit(solution)/shard_map/ppermute | solution.py:346
  179.3 0.1 add_convert_fusion.7
  179.4 4.1 %collective-permute-done.246 = bf16[96,1024]{1,0:T(8,128)(2,1)S(1)} collective-permute-done((bf16[96,1024]{1,0:T(8,128)(2,1)S(1)}, bf16[96,1024]{1,0:T(8,128)(2,1)S(1)}, u32[]{:S(2)}, u32[]{:S(2)}) %collective-permute-start.246) | collective-permute-done | bytes 196640 | tf_op jit(solution)/shard_map/ppermute | solution.py:346
  183.5 0.1 add_convert_fusion
  183.6 0.8 pad_maximum_fusion.1
  (28 shorter events, 0.2 us)
Async XLA Ops:
  3.2 11.6 %collective-permute-start.229 = (bf16[200,1024]{1,0:T(8,128)(2,1)S(1)}, bf16[200,1024]{1,0:T(8,128)(2,1)}, u32[]{:S(2)}, u32[]{:S(2)}) collective-permute-start(bf16[200,1024]{1,0:T(8,128)(2,1)S(1)} %fusion.7.refs_0_), channel_id=1, source_target_pairs={{0,2},{2,4},{4,6},{6,7},{7,5},{5,3},{3,1},{1,0},{8,10},{10,12},{12... | collective-permute-start | bytes 1228808 | tf_op jit(solution)/shard_map/ppermute | solution.py:293
  5.3 10.2 %collective-permute-start.230 = (bf16[200,1024]{1,0:T(8,128)(2,1)S(1)}, bf16[200,1024]{1,0:T(8,128)(2,1)}, u32[]{:S(2)}, u32[]{:S(2)}) collective-permute-start(bf16[200,1024]{1,0:T(8,128)(2,1)S(1)} %fusion.7.refs_0_), channel_id=1, source_target_pairs={{2,0},{4,2},{6,4},{7,6},{5,7},{3,5},{1,3},{0,1},{10,8},{12,10},{14... | collective-permute-start | bytes 1228808 | tf_op jit(solution)/shard_map/ppermute | solution.py:293
  9.3 5.3 %copy-start.3 = (s32[8]{0:T(128)S(1)}, s32[8]{0:T(128)}, u32[]{:S(2)}) copy-start(s32[8]{0:T(128)} %param.40) | copy-start | bytes 100
  9.3 5.3 %copy-start.4 = (s32[8]{0:T(128)S(1)}, s32[8]{0:T(128)}, u32[]{:S(2)}) copy-start(s32[8]{0:T(128)} %param.41) | copy-start | bytes 100
  9.3 6.2 %copy-start.2 = (bf16[1,3,1024,256]{3,2,1,0:T(8,128)(2,1)S(1)}, bf16[1,3,1024,256]{3,2,1,0:T(8,128)(2,1)}, u32[]{:S(2)}) copy-start(bf16[1,3,1024,256]{3,2,1,0:T(8,128)(2,1)} %refs_0_.1) | copy-start | bytes 4718596
  15.5 43.9 %collective-permute-start.33 = (bf16[2,3,1024,256]{3,2,1,0:T(8,128)(2,1)}, bf16[2,3,1024,256]{3,2,1,0:T(8,128)(2,1)}, u32[]{:S(2)}, u32[]{:S(2)}) collective-permute-start(bf16[2,3,1024,256]{3,2,1,0:T(8,128)(2,1)} %get-tuple-element.259), channel_id=1, source_target_pairs={{1,3},{3,1},{17,19},{19,17},{9,8},{11,10},{25,24},{27,26}} | collective-permute-start | bytes 9437192 | tf_op jit(solution)/shard_map/cond/branch_4_fun/ppermute | solution.py:44
  22.4 44.7 %collective-permute-start.37 = (bf16[1,3,1024,256]{3,2,1,0:T(8,128)(2,1)S(1)}, bf16[1,3,1024,256]{3,2,1,0:T(8,128)(2,1)}, u32[]{:S(2)}, u32[]{:S(2)}) collective-permute-start(bf16[1,3,1024,256]{3,2,1,0:T(8,128)(2,1)S(1)} %get-tuple-element.258), channel_id=1, source_target_pairs={{0,16},{8,24},{16,0},{24,8},{1,17},{9,25},{17,1},{25,9},{2,18},{10... | collective-permute-start | bytes 4718600 | tf_op jit(solution)/shard_map/cond/branch_4_fun/ppermute | solution.py:306
  23.8 43.4 %collective-permute-start.38 = (bf16[1,3,1024,256]{3,2,1,0:T(8,128)(2,1)S(1)}, bf16[1,3,1024,256]{3,2,1,0:T(8,128)(2,1)}, u32[]{:S(2)}, u32[]{:S(2)}) collective-permute-start(bf16[1,3,1024,256]{3,2,1,0:T(8,128)(2,1)S(1)} %get-tuple-element.258), channel_id=1, source_target_pairs={{0,8},{8,0},{16,24},{24,16},{1,9},{9,1},{17,25},{25,17},{2,10},{10... | collective-permute-start | bytes 4718600 | tf_op jit(solution)/shard_map/cond/branch_4_fun/ppermute | solution.py:303
  59.4 46.4 %collective-permute-start.34 = (bf16[2,3,1024,256]{3,2,1,0:T(8,128)(2,1)}, bf16[2,3,1024,256]{3,2,1,0:T(8,128)(2,1)}, u32[]{:S(2)}, u32[]{:S(2)}) collective-permute-start(bf16[2,3,1024,256]{3,2,1,0:T(8,128)(2,1)} %collective-permute-done.33), channel_id=1, source_target_pairs={{8,11},{10,9},{24,27},{26,25}} | collective-permute-start | bytes 9437192 | tf_op jit(solution)/shard_map/cond/branch_4_fun/ppermute | solution.py:46
  63.4 42.4 %collective-permute-start.32 = (bf16[1,3,1024,256]{3,2,1,0:T(8,128)(2,1)S(1)}, bf16[1,3,1024,256]{3,2,1,0:T(8,128)(2,1)}, u32[]{:S(2)}, u32[]{:S(2)}) collective-permute-start(bf16[1,3,1024,256]{3,2,1,0:T(8,128)(2,1)S(1)} %get-tuple-element.258), channel_id=1, source_target_pairs={{1,3},{3,1},{17,19},{19,17},{9,11},{11,9},{25,27},{27,25}} | collective-permute-start | bytes 4718600 | tf_op jit(solution)/shard_map/cond/branch_4_fun/ppermute | solution.py:45
  67.1 38.6 %collective-permute-start.39 = (bf16[1,3,1024,256]{3,2,1,0:T(8,128)(2,1)}, bf16[1,3,1024,256]{3,2,1,0:T(8,128)(2,1)}, u32[]{:S(2)}, u32[]{:S(2)}) collective-permute-start(bf16[1,3,1024,256]{3,2,1,0:T(8,128)(2,1)} %collective-permute-done.37), channel_id=1, source_target_pairs={{0,8},{8,0},{16,24},{24,16},{1,9},{9,1},{17,25},{25,17},{2,10},{10... | collective-permute-start | bytes 4718600 | tf_op jit(solution)/shard_map/cond/branch_4_fun/ppermute | solution.py:308
  67.3 37.7 %collective-permute-start.35 = (bf16[200,1024]{1,0:T(8,128)(2,1)}, bf16[200,1024]{1,0:T(8,128)(2,1)}, u32[]{:S(2)}, u32[]{:S(2)}) collective-permute-start(bf16[200,1024]{1,0:T(8,128)(2,1)} %get-tuple-element.260), channel_id=1, source_target_pairs={{0,2},{2,4},{4,6},{6,7},{7,5},{5,3},{3,1},{1,0},{8,10},{10,12},{12... | collective-permute-start | bytes 1228808 | tf_op jit(solution)/shard_map/cond/branch_4_fun/ppermute | solution.py:293
  68.9 36.9 %collective-permute-start.36 = (bf16[200,1024]{1,0:T(8,128)(2,1)}, bf16[200,1024]{1,0:T(8,128)(2,1)}, u32[]{:S(2)}, u32[]{:S(2)}) collective-permute-start(bf16[200,1024]{1,0:T(8,128)(2,1)} %get-tuple-element.261), channel_id=1, source_target_pairs={{2,0},{4,2},{6,4},{7,6},{5,7},{3,5},{1,3},{0,1},{10,8},{12,10},{14... | collective-permute-start | bytes 1228808 | tf_op jit(solution)/shard_map/cond/branch_4_fun/ppermute | solution.py:293
  106.1 15.8 %collective-permute-start.231 = (bf16[200,1024]{1,0:T(8,128)(2,1)}, bf16[200,1024]{1,0:T(8,128)(2,1)S(1)}, u32[]{:S(2)}, u32[]{:S(2)}) collective-permute-start(bf16[200,1024]{1,0:T(8,128)(2,1)} %get-tuple-element.446.refs_0_), channel_id=1, source_target_pairs={{0,2},{2,4},{4,6},{6,7},{7,5},{5,3},{3,1},{1,0},{8,10},{10,12},{12... | collective-permute-start | bytes 1228808 | tf_op jit(solution)/shard_map/ppermute | solution.py:293
  107.3 14.6 %collective-permute-start.232 = (bf16[200,1024]{1,0:T(8,128)(2,1)}, bf16[200,1024]{1,0:T(8,128)(2,1)S(1)}, u32[]{:S(2)}, u32[]{:S(2)}) collective-permute-start(bf16[200,1024]{1,0:T(8,128)(2,1)} %get-tuple-element.447.refs_1_), channel_id=1, source_target_pairs={{2,0},{4,2},{6,4},{7,6},{5,7},{3,5},{1,3},{0,1},{10,8},{12,10},{14... | collective-permute-start | bytes 1228808 | tf_op jit(solution)/shard_map/ppermute | solution.py:293
  122.6 7.3 %collective-permute-start.233 = (bf16[200,1024]{1,0:T(8,128)(2,1)}, bf16[200,1024]{1,0:T(8,128)(2,1)S(1)}, u32[]{:S(2)}, u32[]{:S(2)}) collective-permute-start(bf16[200,1024]{1,0:T(8,128)(2,1)} %broadcast_select_fusion.1), channel_id=1, source_target_pairs={{0,2},{2,4},{4,6},{6,7},{7,5},{5,3},{3,1},{1,0},{10,8},{12,10},{14... | collective-permute-start | bytes 1228808 | tf_op jit(solution)/shard_map/ppermute | solution.py:332
  133.5 17.1 %collective-permute-start.234 = (bf16[192,1024]{1,0:T(8,128)(2,1)S(1)}, bf16[192,1024]{1,0:T(8,128)(2,1)S(1)}, u32[]{:S(2)}, u32[]{:S(2)}) collective-permute-start(bf16[192,1024]{1,0:T(8,128)(2,1)S(1)} %shard_map.115), channel_id=1, source_target_pairs={{0,2},{2,4},{4,6},{6,7},{7,5},{5,3},{3,1},{1,0},{10,8},{12,10},{14... | collective-permute-start | bytes 1179656 | tf_op jit(solution)/shard_map/ppermute | solution.py:336
  134.7 7.1 %copy-start = (f32[1,3,1024,256]{3,2,1,0:T(8,128)S(1)}, f32[1,3,1024,256]{3,2,1,0:T(8,128)}, u32[]{:S(2)}) copy-start(f32[1,3,1024,256]{3,2,1,0:T(8,128)} %refs_1_.3) | copy-start | bytes 9437188
  134.7 7.1 %copy-start.1 = (f32[1,3,1024,256]{3,2,1,0:T(8,128)S(1)}, f32[1,3,1024,256]{3,2,1,0:T(8,128)}, u32[]{:S(2)}) copy-start(f32[1,3,1024,256]{3,2,1,0:T(8,128)} %refs_2_.5) | copy-start | bytes 9437188
  150.9 8.8 %collective-permute-start.235 = (bf16[96,1024]{1,0:T(8,128)(2,1)S(1)}, bf16[96,1024]{1,0:T(8,128)(2,1)S(1)}, u32[]{:S(2)}, u32[]{:S(2)}) collective-permute-start(bf16[96,1024]{1,0:T(8,128)(2,1)S(1)} %get-tuple-element.474), channel_id=1, source_target_pairs={{2,0},{4,2},{6,4},{7,6},{5,7},{3,5},{1,3},{0,1},{10,8},{12,10},{14... | collective-permute-start | bytes 589832 | tf_op jit(solution)/shard_map/ppermute | solution.py:345
  158.0 4.6 %collective-permute-start.238 = (bf16[96,1024]{1,0:T(8,128)(2,1)S(1)}, bf16[96,1024]{1,0:T(8,128)(2,1)S(1)}, u32[]{:S(2)}, u32[]{:S(2)}) collective-permute-start(bf16[96,1024]{1,0:T(8,128)(2,1)S(1)} %get-tuple-element.475), channel_id=1, source_target_pairs={{0,2},{2,4},{4,6},{6,7},{7,5},{5,3},{3,1},{1,0},{8,10},{10,12},{12... | collective-permute-start | bytes 589832 | tf_op jit(solution)/shard_map/ppermute | solution.py:346
  158.1 4.9 %collective-permute-start.241 = (bf16[96,1024]{1,0:T(8,128)(2,1)S(1)}, bf16[96,1024]{1,0:T(8,128)(2,1)S(1)}, u32[]{:S(2)}, u32[]{:S(2)}) collective-permute-start(bf16[96,1024]{1,0:T(8,128)(2,1)S(1)} %get-tuple-element.477), channel_id=1, source_target_pairs={{2,0},{4,2},{6,4},{7,6},{5,7},{3,5},{1,3},{0,1},{10,8},{12,10},{14... | collective-permute-start | bytes 589832 | tf_op jit(solution)/shard_map/ppermute | solution.py:345
  159.6 7.1 %collective-permute-start.244 = (bf16[96,1024]{1,0:T(8,128)(2,1)S(1)}, bf16[96,1024]{1,0:T(8,128)(2,1)S(1)}, u32[]{:S(2)}, u32[]{:S(2)}) collective-permute-start(bf16[96,1024]{1,0:T(8,128)(2,1)S(1)} %get-tuple-element.476), channel_id=1, source_target_pairs={{0,2},{2,4},{4,6},{6,7},{7,5},{5,3},{3,1},{1,0},{8,10},{10,12},{12... | collective-permute-start | bytes 589832 | tf_op jit(solution)/shard_map/ppermute | solution.py:346
  159.7 7.4 %collective-permute-start.236 = (bf16[96,1024]{1,0:T(8,128)(2,1)S(1)}, bf16[96,1024]{1,0:T(8,128)(2,1)S(1)}, u32[]{:S(2)}, u32[]{:S(2)}) collective-permute-start(bf16[96,1024]{1,0:T(8,128)(2,1)S(1)} %add_convert_fusion.12), channel_id=1, source_target_pairs={{2,0},{4,2},{6,4},{7,6},{5,7},{3,5},{1,3},{0,1},{10,8},{12,10},{14... | collective-permute-start | bytes 589832 | tf_op jit(solution)/shard_map/ppermute | solution.py:345
  162.7 8.2 %collective-permute-start.239 = (bf16[96,1024]{1,0:T(8,128)(2,1)S(1)}, bf16[96,1024]{1,0:T(8,128)(2,1)S(1)}, u32[]{:S(2)}, u32[]{:S(2)}) collective-permute-start(bf16[96,1024]{1,0:T(8,128)(2,1)S(1)} %add_convert_fusion.9), channel_id=1, source_target_pairs={{0,2},{2,4},{4,6},{6,7},{7,5},{5,3},{3,1},{1,0},{8,10},{10,12},{12... | collective-permute-start | bytes 589832 | tf_op jit(solution)/shard_map/ppermute | solution.py:346
  163.1 8.2 %collective-permute-start.242 = (bf16[96,1024]{1,0:T(8,128)(2,1)S(1)}, bf16[96,1024]{1,0:T(8,128)(2,1)S(1)}, u32[]{:S(2)}, u32[]{:S(2)}) collective-permute-start(bf16[96,1024]{1,0:T(8,128)(2,1)S(1)} %add_convert_fusion.5), channel_id=1, source_target_pairs={{2,0},{4,2},{6,4},{7,6},{5,7},{3,5},{1,3},{0,1},{10,8},{12,10},{14... | collective-permute-start | bytes 589832 | tf_op jit(solution)/shard_map/ppermute | solution.py:345
  166.7 8.4 %collective-permute-start.245 = (bf16[96,1024]{1,0:T(8,128)(2,1)S(1)}, bf16[96,1024]{1,0:T(8,128)(2,1)S(1)}, u32[]{:S(2)}, u32[]{:S(2)}) collective-permute-start(bf16[96,1024]{1,0:T(8,128)(2,1)S(1)} %add_convert_fusion.2), channel_id=1, source_target_pairs={{0,2},{2,4},{4,6},{6,7},{7,5},{5,3},{3,1},{1,0},{8,10},{10,12},{12... | collective-permute-start | bytes 589832 | tf_op jit(solution)/shard_map/ppermute | solution.py:346
  167.1 8.4 %collective-permute-start.237 = (bf16[96,1024]{1,0:T(8,128)(2,1)S(1)}, bf16[96,1024]{1,0:T(8,128)(2,1)S(1)}, u32[]{:S(2)}, u32[]{:S(2)}) collective-permute-start(bf16[96,1024]{1,0:T(8,128)(2,1)S(1)} %add_convert_fusion.11), channel_id=1, source_target_pairs={{2,0},{4,2},{6,4},{7,6},{5,7},{3,5},{1,3},{0,1},{10,8},{12,10},{14... | collective-permute-start | bytes 589832 | tf_op jit(solution)/shard_map/ppermute | solution.py:345
  171.0 8.4 %collective-permute-start.240 = (bf16[96,1024]{1,0:T(8,128)(2,1)S(1)}, bf16[96,1024]{1,0:T(8,128)(2,1)S(1)}, u32[]{:S(2)}, u32[]{:S(2)}) collective-permute-start(bf16[96,1024]{1,0:T(8,128)(2,1)S(1)} %add_convert_fusion.8), channel_id=1, source_target_pairs={{0,2},{2,4},{4,6},{6,7},{7,5},{5,3},{3,1},{1,0},{8,10},{10,12},{12... | collective-permute-start | bytes 589832 | tf_op jit(solution)/shard_map/ppermute | solution.py:346
  171.4 8.1 %collective-permute-start.243 = (bf16[96,1024]{1,0:T(8,128)(2,1)S(1)}, bf16[96,1024]{1,0:T(8,128)(2,1)S(1)}, u32[]{:S(2)}, u32[]{:S(2)}) collective-permute-start(bf16[96,1024]{1,0:T(8,128)(2,1)S(1)} %add_convert_fusion.4), channel_id=1, source_target_pairs={{2,0},{4,2},{6,4},{7,6},{5,7},{3,5},{1,3},{0,1},{10,8},{12,10},{14... | collective-permute-start | bytes 589832 | tf_op jit(solution)/shard_map/ppermute | solution.py:345
  175.2 8.4 %collective-permute-start.246 = (bf16[96,1024]{1,0:T(8,128)(2,1)S(1)}, bf16[96,1024]{1,0:T(8,128)(2,1)S(1)}, u32[]{:S(2)}, u32[]{:S(2)}) collective-permute-start(bf16[96,1024]{1,0:T(8,128)(2,1)S(1)} %add_convert_fusion.1), channel_id=1, source_target_pairs={{0,2},{2,4},{4,6},{6,7},{7,5},{5,3},{3,1},{1,0},{8,10},{10,12},{12... | collective-permute-start | bytes 589832 | tf_op jit(solution)/shard_map/ppermute | solution.py:346
where the time goes:
time: 188 us; the launch traced here: 184 us
  waiting for transfers between devices  102 us (54%)
  starting transfers between devices  41.4 us (22%)
  Pallas kernels  29.9 us (16%)
  other arithmetic  7.1 us (4%)
  between operations  4.1 us (2%)
    ppermute x3, waiting for transfers between devices, hop(): lax.ppermute(back, 'expert', ahead)  45.1 us
    ppermute x1, waiting for transfers between devices, swap_slots(): direct = lax.ppermute(moments, axes, spread(0, swap) + first_hop)  33.3 us
    pallas_call x4, Pallas kernels, run_expert(): pl.pallas_call(functools.partial(expert_kernel, blocks, len(shards), tok_...  20.3 us
    ppermute x6, waiting for transfers between devices, whole(): to_ahead = lax.ppermute(front, 'expert', ahead).astype(jnp.float32)  16.9 us
    ppermute x6, starting transfers between devices, whole(): to_behind = lax.ppermute(back, 'expert', behind).astype(jnp.float32)  8.34 us
    ppermute x1, starting transfers between devices, swap_slots(): direct = lax.ppermute(moments, axes, spread(0, swap) + first_hop)  6.91 us
    ppermute x3, starting transfers between devices, hop(): lax.ppermute(front, 'expert', behind)  5.55 us
    pallas_call x1, Pallas kernels, pack_moments(): pl.pallas_call(pack_kernel, grid=(parts,), out_shape=jax.ShapeDtypeStruct...  5.28 us
  transfers between devices with their start and end apart: 26, of which 12 were waited for; matrix products, arithmetic and copies ran while one was open for 1% of the time, Pallas kernels for 14%

commit v1 on v0

--- a/solution.py
+++ b/solution.py
@@ -344,8 +344,9 @@
             front = (answers[step][2 + half] + to_ahead).astype(jnp.bfloat16)
             to_behind = lax.ppermute(back, "expert", behind).astype(jnp.float32)
             to_ahead = lax.ppermute(front, "expert", ahead).astype(jnp.float32)
-        outputs.append((own[half] + to_behind + to_ahead).astype(jnp.bfloat16))
-    layer_output = jnp.concatenate(outputs, axis=0)
+        outputs.append((to_behind, to_ahead, own[half]))
+    back, front, kept = (jnp.concatenate(parts, axis=0) for parts in zip(*outputs))
+    layer_output = (kept + back + front).astype(jnp.bfloat16)
 
     here = jnp.sum(jnp.where(labels == slot, source_slot, 0)) != slot
     flags = jnp.stack([here, odd]).astype(jnp.int32)

time: 188 us -> 186 us (0.989)
  the two profiles are of different devices: /device:TPU:1 before, /device:TPU:0 now
where the time goes in v1:
time: 186 us
  starting transfers between devices  76 us (41%)
  waiting for transfers between devices  62.5 us (34%)
  Pallas kernels  29.7 us (16%)
  other arithmetic  11 us (6%)
  between operations  4.13 us (2%)
  local copies, waits for them, and re-layouts  1.93 us (1%)
    ppermute x1, starting transfers between devices, swap_slots(): lax.ppermute(weights, axes, spread(0, swap) + spread(1, swap))  38.8 us
    ppermute x3, waiting for transfers between devices, hop(): lax.ppermute(front, 'expert', behind)  27.5 us
    pallas_call x4, Pallas kernels, run_expert(): pl.pallas_call(functools.partial(expert_kernel, blocks, len(shards), tok_...  19.7 us
    ppermute x3, waiting for transfers between devices, hop(): lax.ppermute(back, 'expert', ahead)  19.2 us
    ppermute x3, starting transfers between devices, hop(): lax.ppermute(front, 'expert', behind)  8.69 us
    ppermute x1, waiting for transfers between devices, whole(): lax.ppermute(jnp.where(odd, *hops[steps - 1][::-1]), ('dp', 'expert'), op...  8.16 us
    ppermute x6, starting transfers between devices, whole(): to_ahead = lax.ppermute(front, 'expert', ahead).astype(jnp.float32)  7.79 us
    ppermute x1, starting transfers between devices, swap_slots(): direct = lax.ppermute(moments, axes, spread(0, swap) + first_hop)  6.86 us
  transfers between devices with their start and end apart: 26, of which 9 were waited for; matrix products, arithmetic and copies ran while one was open for 3% of the time, Pallas kernels for 14%

profile of v1, /device:TPU:0, one launch (start us, length us, event | category | flops | bytes accessed | tf_op | source)
XLA Modules:
  0.0 185.5 jit_solution(6409957901351942872)
XLA Ops:
  0.6 0.7 iota_compare_fusion.5
  1.3 0.7 select_reduce_fusion.1
  2.0 0.1 select_reduce_fusion
  2.1 1.0 fusion.9.refs_0_
  3.2 3.1 %collective-permute-start.229 = (bf16[200,1024]{1,0:T(8,128)(2,1)S(1)}, bf16[200,1024]{1,0:T(8,128)(2,1)}, u32[]{:S(2)}, u32[]{:S(2)}) collective-permute-start(bf16[200,1024]{1,0:T(8,128)(2,1)S(1)} %fusion.9.refs_0_), channel_id=1, source_target_pairs={{0,2},{2,4},{4,6},{6,7},{7,5},{5,3},{3,1},{1,0},{8,10},{10,12},{12... | collective-permute-start | bytes 1228808 | tf_op jit(solution)/shard_map/ppermute | solution.py:293
  6.3 0.0 collective-permute-start.230
  6.3 1.3 select_reduce_fusion.3
  10.2 0.0 copy-start.6
  10.2 0.0 copy-start.7
  10.2 0.0 copy-start.4
  10.2 5.3 %shard_map.111 = bf16[2,3,1024,256]{3,2,1,0:T(8,128)(2,1)} custom-call(f32[1,3,1024,256]{3,2,1,0:T(8,128)} %refs_1_.3, f32[1,3,1024,256]{3,2,1,0:T(8,128)} %refs_2_.5), custom_call_target="tpu_custom_call" | custom-call | flops 786432 | bytes 9437184 | tf_op jit(solution)/shard_map/pallas_call | solution.py:69
  15.5 0.1 select_reduce_fusion.2
  15.6 0.1 collective-permute-done.229.refs_1_
  15.8 1.5 collective-permute-done.230.refs_2_
  17.3 88.4 %conditional.1 = (bf16[1,3,1024,256]{3,2,1,0:T(8,128)(2,1)}, bf16[2,3,1024,256]{3,2,1,0:T(8,128)(2,1)}, bf16[2,3,1024,256]{3,2,1,0:T(8,128)(2,1)}, bf16[200,1024...) conditional(s32[]{:T(128)} %clamp.3, ...), branch_computations={%region_6.7_spmd, %region_7.8_spmd, %region_8.9_spmd, %region_9.10... | conditional | flops 11797576 | bytes 94507512 | solution.py:182
  17.3 6.9 %collective-permute-start.33 = (bf16[2,3,1024,256]{3,2,1,0:T(8,128)(2,1)}, bf16[2,3,1024,256]{3,2,1,0:T(8,128)(2,1)}, u32[]{:S(2)}, u32[]{:S(2)}) collective-permute-start(bf16[2,3,1024,256]{3,2,1,0:T(8,128)(2,1)} %get-tuple-element.259), channel_id=1, source_target_pairs={{1,3},{3,1},{17,19},{19,17},{9,8},{11,10},{25,24},{27,26}} | collective-permute-start | bytes 9437192 | tf_op jit(solution)/shard_map/cond/branch_4_fun/ppermute | solution.py:44
  24.2 1.9 %collective-permute-start.37 = (bf16[1,3,1024,256]{3,2,1,0:T(8,128)(2,1)S(1)}, bf16[1,3,1024,256]{3,2,1,0:T(8,128)(2,1)}, u32[]{:S(2)}, u32[]{:S(2)}) collective-permute-start(bf16[1,3,1024,256]{3,2,1,0:T(8,128)(2,1)S(1)} %get-tuple-element.258), channel_id=1, source_target_pairs={{0,16},{8,24},{16,0},{24,8},{1,17},{9,25},{17,1},{25,9},{2,18},{10... | collective-permute-start | bytes 4718600 | tf_op jit(solution)/shard_map/cond/branch_4_fun/ppermute | solution.py:306
  26.0 0.0 collective-permute-done.33
  26.1 2.3 %collective-permute-start.34 = (bf16[2,3,1024,256]{3,2,1,0:T(8,128)(2,1)}, bf16[2,3,1024,256]{3,2,1,0:T(8,128)(2,1)}, u32[]{:S(2)}, u32[]{:S(2)}) collective-permute-start(bf16[2,3,1024,256]{3,2,1,0:T(8,128)(2,1)} %collective-permute-done.33), channel_id=1, source_target_pairs={{8,11},{10,9},{24,27},{26,25}} | collective-permute-start | bytes 9437192 | tf_op jit(solution)/shard_map/cond/branch_4_fun/ppermute | solution.py:46
  28.4 38.8 %collective-permute-start.32 = (bf16[1,3,1024,256]{3,2,1,0:T(8,128)(2,1)S(1)}, bf16[1,3,1024,256]{3,2,1,0:T(8,128)(2,1)}, u32[]{:S(2)}, u32[]{:S(2)}) collective-permute-start(bf16[1,3,1024,256]{3,2,1,0:T(8,128)(2,1)S(1)} %get-tuple-element.258), channel_id=1, source_target_pairs={{1,3},{3,1},{17,19},{19,17},{9,11},{11,9},{25,27},{27,25}} | collective-permute-start | bytes 4718600 | tf_op jit(solution)/shard_map/cond/branch_4_fun/ppermute | solution.py:45
  67.2 0.4 collective-permute-start.39
  67.6 1.6 collective-permute-start.35
  69.2 0.4 collective-permute-start.36
  69.6 9.8 %collective-permute-done.35 = bf16[200,1024]{1,0:T(8,128)(2,1)} collective-permute-done((bf16[200,1024]{1,0:T(8,128)(2,1)}, bf16[200,1024]{1,0:T(8,128)(2,1)}, u32[]{:S(2)}, u32[]{:S(2)}) %collective-permute-start.35) | collective-permute-done | bytes 409632 | tf_op jit(solution)/shard_map/cond/branch_4_fun/ppermute | solution.py:293
  79.4 26.0 %collective-permute-done.36 = bf16[200,1024]{1,0:T(8,128)(2,1)} collective-permute-done((bf16[200,1024]{1,0:T(8,128)(2,1)}, bf16[200,1024]{1,0:T(8,128)(2,1)}, u32[]{:S(2)}, u32[]{:S(2)}) %collective-permute-start.36) | collective-permute-done | bytes 409632 | tf_op jit(solution)/shard_map/cond/branch_4_fun/ppermute | solution.py:293
  105.4 0.0 collective-permute-done.32
  105.4 0.0 collective-permute-done.39
  105.7 0.1 collective-permute-start.231
  105.7 8.3 %collective-permute-start.232 = (bf16[200,1024]{1,0:T(8,128)(2,1)}, bf16[200,1024]{1,0:T(8,128)(2,1)S(1)}, u32[]{:S(2)}, u32[]{:S(2)}) collective-permute-start(bf16[200,1024]{1,0:T(8,128)(2,1)} %get-tuple-element.448.refs_1_), channel_id=1, source_target_pairs={{2,0},{4,2},{6,4},{7,6},{5,7},{3,5},{1,3},{0,1},{10,8},{12,10},{14... | collective-permute-start | bytes 1228808 | tf_op jit(solution)/shard_map/ppermute | solution.py:293
  114.0 9.3 %collective-permute-done.231.refs_0_ = bf16[200,1024]{1,0:T(8,128)(2,1)S(1)} collective-permute-done((bf16[200,1024]{1,0:T(8,128)(2,1)}, bf16[200,1024]{1,0:T(8,128)(2,1)S(1)}, u32[]{:S(2)}, u32[]{:S(2)}) %collective-permute-start.231) | collective-permute-done | bytes 409632 | tf_op jit(solution)/shard_map/ppermute | solution.py:293
  123.4 0.8 broadcast_select_fusion.1
  124.2 8.2 %collective-permute-done.233.refs_0_ = bf16[200,1024]{1,0:T(8,128)(2,1)S(1)} collective-permute-done((bf16[200,1024]{1,0:T(8,128)(2,1)}, bf16[200,1024]{1,0:T(8,128)(2,1)S(1)}, u32[]{:S(2)}, u32[]{:S(2)}) %collective-permute-start.233) | collective-permute-done | bytes 409632 | tf_op jit(solution)/shard_map/ppermute | solution.py:332
  132.3 3.6 %shard_map.115 = bf16[192,1024]{1,0:T(8,128)(2,1)S(1)} custom-call(s32[1]{0:T(128)} %bitcast.4.slot_ref, bf16[200,1024]{1,0:T(8,128)(2,1)S(1)} %collective-permute-done.233.refs_0_, bf16[1,3,1024,256]{3,2,1,0:T(8,128)(2,1)S(1)} %copy-done.4, bf16[1,3,1024,256]{3,2,1,0:T(8,128)(2,1)} %get-tuple-element.441.refs_4_.refs_3_.refs_2_, ...), custom_call_target="tpu_custom_call" | custom-call | flops 1207959552 | bytes 7471104 | tf_op jit(solution)/shard_map/pallas_call | solution.py:234
  135.9 0.1 collective-permute-start.234
  136.0 6.3 %shard_map.112 = (f32[96,1024]{1,0:T(8,128)S(1)}, f32[96,1024]{1,0:T(8,128)S(1)}, f32[96,1024]{1,0:T(8,128)S(1)}, f32[96,1024]{1,0:T(8,128)S(1)}, f32[96,1024]{1,0:T(8,128)S(1)}, /*index=5*/f32[96,1024]{1,0:T(8,128)S(1)}) custom-call(s32[1]{0:T(128)} %bitcast.4.slot_ref, bf16[200,1024]{1,0:T(8,128)(2,1)S(1)} %fusion.9.refs_0_, ...), custom_call_target="tpu_custom_call" | custom-call | flops 3623878656 | bytes 9830400 | tf_op jit(solution)/shard_map/pallas_call | solution.py:234
  142.3 0.0 copy-start.2
  142.3 4.3 %shard_map.114 = (f32[96,1024]{1,0:T(8,128)S(1)}, f32[96,1024]{1,0:T(8,128)S(1)}, f32[96,1024]{1,0:T(8,128)S(1)}, f32[96,1024]{1,0:T(8,128)S(1)}) custom-call(s32[1]{0:T(128)} %bitcast.4.slot_ref, bf16[200,1024]{1,0:T(8,128)(2,1)S(1)} %collective-permute-done.231.refs_0_, bf16[200,1024]{1,0:T(8,128)(2,1)S(1)} %collective-permute-done.232.refs_1_, ...), custom_call_target="tpu_custom_call" | custom-call | flops 2415919104 | bytes 8650752 | tf_op jit(solution)/shard_map/pallas_call | solution.py:234
  146.7 0.1 convert_element_type.93
  146.8 0.3 add_convert_fusion.5
  147.0 0.1 collective-permute-start.241
  147.1 5.4 %shard_map.113 = (f32[96,1024]{1,0:T(8,128)S(1)}, f32[96,1024]{1,0:T(8,128)S(1)}, f32[96,1024]{1,0:T(8,128)S(1)}, f32[96,1024]{1,0:T(8,128)S(1)}) custom-call(s32[1]{0:T(128)} %bitcast.4.slot_ref, bf16[200,1024]{1,0:T(8,128)(2,1)} %get-tuple-element.447.refs_0_, bf16[200,1024]{1,0:T(8,128)(2,1)} %get-tuple-element.448.refs_1_, ...), custom_call_target="tpu_custom_call" | custom-call | flops 2415919104 | bytes 8650752 | tf_op jit(solution)/shard_map/pallas_call | solution.py:234
  152.5 1.9 %collective-permute-start.244 = (bf16[96,1024]{1,0:T(8,128)(2,1)S(1)}, bf16[96,1024]{1,0:T(8,128)(2,1)S(1)}, u32[]{:S(2)}, u32[]{:S(2)}) collective-permute-start(bf16[96,1024]{1,0:T(8,128)(2,1)S(1)} %get-tuple-element.475), channel_id=1, source_target_pairs={{0,2},{2,4},{4,6},{6,7},{7,5},{5,3},{3,1},{1,0},{8,10},{10,12},{12... | collective-permute-start | bytes 589832 | tf_op jit(solution)/shard_map/ppermute | solution.py:346
  154.5 0.2 collective-permute-start.235
  154.6 2.0 %collective-permute-start.238 = (bf16[96,1024]{1,0:T(8,128)(2,1)S(1)}, bf16[96,1024]{1,0:T(8,128)(2,1)S(1)}, u32[]{:S(2)}, u32[]{:S(2)}) collective-permute-start(bf16[96,1024]{1,0:T(8,128)(2,1)S(1)} %get-tuple-element.476), channel_id=1, source_target_pairs={{2,0},{4,2},{6,4},{7,6},{5,7},{3,5},{1,3},{0,1},{10,8},{12,10},{14... | collective-permute-start | bytes 589832 | tf_op jit(solution)/shard_map/ppermute | solution.py:345
  156.7 0.3 collective-permute-start.242
  157.0 3.4 %collective-permute-done.244 = bf16[96,1024]{1,0:T(8,128)(2,1)S(1)} collective-permute-done((bf16[96,1024]{1,0:T(8,128)(2,1)S(1)}, bf16[96,1024]{1,0:T(8,128)(2,1)S(1)}, u32[]{:S(2)}, u32[]{:S(2)}) %collective-permute-start.244) | collective-permute-done | bytes 196640 | tf_op jit(solution)/shard_map/ppermute | solution.py:346
  160.4 2.0 %collective-permute-start.245 = (bf16[96,1024]{1,0:T(8,128)(2,1)S(1)}, bf16[96,1024]{1,0:T(8,128)(2,1)S(1)}, u32[]{:S(2)}, u32[]{:S(2)}) collective-permute-start(bf16[96,1024]{1,0:T(8,128)(2,1)S(1)} %add_convert_fusion.1), channel_id=1, source_target_pairs={{0,2},{2,4},{4,6},{6,7},{7,5},{5,3},{3,1},{1,0},{8,10},{10,12},{12... | collective-permute-start | bytes 589832 | tf_op jit(solution)/shard_map/ppermute | solution.py:346
  162.4 0.2 collective-permute-start.236
  162.5 3.4 %collective-permute-done.238 = bf16[96,1024]{1,0:T(8,128)(2,1)S(1)} collective-permute-done((bf16[96,1024]{1,0:T(8,128)(2,1)S(1)}, bf16[96,1024]{1,0:T(8,128)(2,1)S(1)}, u32[]{:S(2)}, u32[]{:S(2)}) %collective-permute-start.238) | collective-permute-done | bytes 196640 | tf_op jit(solution)/shard_map/ppermute | solution.py:345
  166.0 0.7 collective-permute-start.239
  166.7 0.7 add_convert_fusion.3
  167.4 1.6 collective-permute-start.243
  169.0 0.7 add_convert_fusion
  169.8 2.0 %collective-permute-start.246 = (bf16[96,1024]{1,0:T(8,128)(2,1)}, bf16[96,1024]{1,0:T(8,128)(2,1)}, u32[]{:S(2)}, u32[]{:S(2)}) collective-permute-start(bf16[96,1024]{1,0:T(8,128)(2,1)} %add_convert_fusion), channel_id=1, source_target_pairs={{0,2},{2,4},{4,6},{6,7},{7,5},{5,3},{3,1},{1,0},{8,10},{10,12},{12... | collective-permute-start | bytes 589832 | tf_op jit(solution)/shard_map/ppermute | solution.py:346
  171.7 0.7 add_convert_fusion.9
  172.5 0.0 collective-permute-start.237
  172.5 0.8 collective-permute-done.239
  173.3 0.7 add_convert_fusion.6
  174.0 1.2 collective-permute-start.240
  175.3 0.6 fusion.10
  176.6 0.1 add_convert_fusion.12.flags
  176.6 1.9 %copy-done.1 = f32[1,3,1024,256]{3,2,1,0:T(8,128)S(1)} copy-done((f32[1,3,1024,256]{3,2,1,0:T(8,128)S(1)}, f32[1,3,1024,256]{3,2,1,0:T(8,128)}, u32[]{:S(2)}) %copy-start.1) | copy-done | bytes 3145752
  178.5 4.8 %shard_map.116 = (bf16[1,3,1024,256]{3,2,1,0:T(8,128)(2,1)}, f32[1,3,1024,256]{3,2,1,0:T(8,128)}, f32[1,3,1024,256]{3,2,1,0:T(8,128)}) custom-call(s32[2]{0:T(128)S(1)} %add_convert_fusion.12.flags, bf16[1,3,1024,256]{3,2,1,0:T(8,128)(2,1)} %refs_0_.1, f32[1,3,1024,256]{3,2,1,0:T(8,128)S(1)} %copy-done, f32[1,3,1024,256]{3,2,1,0:T(8,128)S(1)} %copy-done.1, ...), custom_call_target="tpu_custom_call" | custom-call | flops 786432 | bytes 15728640 | tf_op jit(solution)/shard_map/pallas_call | solution.py:144
  183.4 2.1 %fusion.7 = bf16[192,1024]{1,0:T(8,128)(2,1)} fusion(f32[96,1024]{1,0:T(8,128)S(1)} %copy-done.3, f32[96,1024]{1,0:T(8,128)S(1)} %get-tuple-element.444, bf16[96,1024]{1,0:T(8,128)(2,1)} %collective-permute-done.240, bf16[96,1024]{1,0:T(8,128)(2,1)} %collective-permute-done.237, bf16[96,1024]{1,0:T(8,128)(2,1)} %collective-permute-done.246, ...), kind=kLoop, calls=%fused_computation.17 | loop fusion | flops 2359296 | bytes 1966080 | tf_op jit(solution)/shard_map/convert_element_type | solution.py:349
  (32 shorter events, 0.2 us)
Async XLA Ops:
  3.2 12.6 %collective-permute-start.229 = (bf16[200,1024]{1,0:T(8,128)(2,1)S(1)}, bf16[200,1024]{1,0:T(8,128)(2,1)}, u32[]{:S(2)}, u32[]{:S(2)}) collective-permute-start(bf16[200,1024]{1,0:T(8,128)(2,1)S(1)} %fusion.9.refs_0_), channel_id=1, source_target_pairs={{0,2},{2,4},{4,6},{6,7},{7,5},{5,3},{3,1},{1,0},{8,10},{10,12},{12... | collective-permute-start | bytes 1228808 | tf_op jit(solution)/shard_map/ppermute | solution.py:293
  6.3 11.0 %collective-permute-start.230 = (bf16[200,1024]{1,0:T(8,128)(2,1)S(1)}, bf16[200,1024]{1,0:T(8,128)(2,1)}, u32[]{:S(2)}, u32[]{:S(2)}) collective-permute-start(bf16[200,1024]{1,0:T(8,128)(2,1)S(1)} %fusion.9.refs_0_), channel_id=1, source_target_pairs={{2,0},{4,2},{6,4},{7,6},{5,7},{3,5},{1,3},{0,1},{10,8},{12,10},{14... | collective-permute-start | bytes 1228808 | tf_op jit(solution)/shard_map/ppermute | solution.py:293
  10.2 5.3 %copy-start.6 = (s32[8]{0:T(128)S(1)}, s32[8]{0:T(128)}, u32[]{:S(2)}) copy-start(s32[8]{0:T(128)} %param.40) | copy-start | bytes 100
  10.2 5.3 %copy-start.7 = (s32[8]{0:T(128)S(1)}, s32[8]{0:T(128)}, u32[]{:S(2)}) copy-start(s32[8]{0:T(128)} %param.41) | copy-start | bytes 100
  10.2 7.1 %copy-start.4 = (bf16[1,3,1024,256]{3,2,1,0:T(8,128)(2,1)S(1)}, bf16[1,3,1024,256]{3,2,1,0:T(8,128)(2,1)}, u32[]{:S(2)}) copy-start(bf16[1,3,1024,256]{3,2,1,0:T(8,128)(2,1)} %refs_0_.1) | copy-start | bytes 4718596
  17.3 8.8 %collective-permute-start.33 = (bf16[2,3,1024,256]{3,2,1,0:T(8,128)(2,1)}, bf16[2,3,1024,256]{3,2,1,0:T(8,128)(2,1)}, u32[]{:S(2)}, u32[]{:S(2)}) collective-permute-start(bf16[2,3,1024,256]{3,2,1,0:T(8,128)(2,1)} %get-tuple-element.259), channel_id=1, source_target_pairs={{1,3},{3,1},{17,19},{19,17},{9,8},{11,10},{25,24},{27,26}} | collective-permute-start | bytes 9437192 | tf_op jit(solution)/shard_map/cond/branch_4_fun/ppermute | solution.py:44
  24.2 43.1 %collective-permute-start.37 = (bf16[1,3,1024,256]{3,2,1,0:T(8,128)(2,1)S(1)}, bf16[1,3,1024,256]{3,2,1,0:T(8,128)(2,1)}, u32[]{:S(2)}, u32[]{:S(2)}) collective-permute-start(bf16[1,3,1024,256]{3,2,1,0:T(8,128)(2,1)S(1)} %get-tuple-element.258), channel_id=1, source_target_pairs={{0,16},{8,24},{16,0},{24,8},{1,17},{9,25},{17,1},{25,9},{2,18},{10... | collective-permute-start | bytes 4718600 | tf_op jit(solution)/shard_map/cond/branch_4_fun/ppermute | solution.py:306
  26.0 41.2 %collective-permute-start.38 = (bf16[1,3,1024,256]{3,2,1,0:T(8,128)(2,1)S(1)}, bf16[1,3,1024,256]{3,2,1,0:T(8,128)(2,1)}, u32[]{:S(2)}, u32[]{:S(2)}) collective-permute-start(bf16[1,3,1024,256]{3,2,1,0:T(8,128)(2,1)S(1)} %get-tuple-element.258), channel_id=1, source_target_pairs={{0,8},{8,0},{16,24},{24,16},{1,9},{9,1},{17,25},{25,17},{2,10},{10... | collective-permute-start | bytes 4718600 | tf_op jit(solution)/shard_map/cond/branch_4_fun/ppermute | solution.py:303
  26.1 79.3 %collective-permute-start.34 = (bf16[2,3,1024,256]{3,2,1,0:T(8,128)(2,1)}, bf16[2,3,1024,256]{3,2,1,0:T(8,128)(2,1)}, u32[]{:S(2)}, u32[]{:S(2)}) collective-permute-start(bf16[2,3,1024,256]{3,2,1,0:T(8,128)(2,1)} %collective-permute-done.33), channel_id=1, source_target_pairs={{8,11},{10,9},{24,27},{26,25}} | collective-permute-start | bytes 9437192 | tf_op jit(solution)/shard_map/cond/branch_4_fun/ppermute | solution.py:46
  28.4 77.0 %collective-permute-start.32 = (bf16[1,3,1024,256]{3,2,1,0:T(8,128)(2,1)S(1)}, bf16[1,3,1024,256]{3,2,1,0:T(8,128)(2,1)}, u32[]{:S(2)}, u32[]{:S(2)}) collective-permute-start(bf16[1,3,1024,256]{3,2,1,0:T(8,128)(2,1)S(1)} %get-tuple-element.258), channel_id=1, source_target_pairs={{1,3},{3,1},{17,19},{19,17},{9,11},{11,9},{25,27},{27,25}} | collective-permute-start | bytes 4718600 | tf_op jit(solution)/shard_map/cond/branch_4_fun/ppermute | solution.py:45
  67.2 38.2 %collective-permute-start.39 = (bf16[1,3,1024,256]{3,2,1,0:T(8,128)(2,1)}, bf16[1,3,1024,256]{3,2,1,0:T(8,128)(2,1)}, u32[]{:S(2)}, u32[]{:S(2)}) collective-permute-start(bf16[1,3,1024,256]{3,2,1,0:T(8,128)(2,1)} %collective-permute-done.37), channel_id=1, source_target_pairs={{0,8},{8,0},{16,24},{24,16},{1,9},{9,1},{17,25},{25,17},{2,10},{10... | collective-permute-start | bytes 4718600 | tf_op jit(solution)/shard_map/cond/branch_4_fun/ppermute | solution.py:308
  67.6 11.8 %collective-permute-start.35 = (bf16[200,1024]{1,0:T(8,128)(2,1)}, bf16[200,1024]{1,0:T(8,128)(2,1)}, u32[]{:S(2)}, u32[]{:S(2)}) collective-permute-start(bf16[200,1024]{1,0:T(8,128)(2,1)} %get-tuple-element.260), channel_id=1, source_target_pairs={{0,2},{2,4},{4,6},{6,7},{7,5},{5,3},{3,1},{1,0},{8,10},{10,12},{12... | collective-permute-start | bytes 1228808 | tf_op jit(solution)/shard_map/cond/branch_4_fun/ppermute | solution.py:293
  69.2 36.1 %collective-permute-start.36 = (bf16[200,1024]{1,0:T(8,128)(2,1)}, bf16[200,1024]{1,0:T(8,128)(2,1)}, u32[]{:S(2)}, u32[]{:S(2)}) collective-permute-start(bf16[200,1024]{1,0:T(8,128)(2,1)} %get-tuple-element.261), channel_id=1, source_target_pairs={{2,0},{4,2},{6,4},{7,6},{5,7},{3,5},{1,3},{0,1},{10,8},{12,10},{14... | collective-permute-start | bytes 1228808 | tf_op jit(solution)/shard_map/cond/branch_4_fun/ppermute | solution.py:293
  105.7 17.7 %collective-permute-start.231 = (bf16[200,1024]{1,0:T(8,128)(2,1)}, bf16[200,1024]{1,0:T(8,128)(2,1)S(1)}, u32[]{:S(2)}, u32[]{:S(2)}) collective-permute-start(bf16[200,1024]{1,0:T(8,128)(2,1)} %get-tuple-element.447.refs_0_), channel_id=1, source_target_pairs={{0,2},{2,4},{4,6},{6,7},{7,5},{5,3},{3,1},{1,0},{8,10},{10,12},{12... | collective-permute-start | bytes 1228808 | tf_op jit(solution)/shard_map/ppermute | solution.py:293
  105.7 17.6 %collective-permute-start.232 = (bf16[200,1024]{1,0:T(8,128)(2,1)}, bf16[200,1024]{1,0:T(8,128)(2,1)S(1)}, u32[]{:S(2)}, u32[]{:S(2)}) collective-permute-start(bf16[200,1024]{1,0:T(8,128)(2,1)} %get-tuple-element.448.refs_1_), channel_id=1, source_target_pairs={{2,0},{4,2},{6,4},{7,6},{5,7},{3,5},{1,3},{0,1},{10,8},{12,10},{14... | collective-permute-start | bytes 1228808 | tf_op jit(solution)/shard_map/ppermute | solution.py:293
  124.1 8.2 %collective-permute-start.233 = (bf16[200,1024]{1,0:T(8,128)(2,1)}, bf16[200,1024]{1,0:T(8,128)(2,1)S(1)}, u32[]{:S(2)}, u32[]{:S(2)}) collective-permute-start(bf16[200,1024]{1,0:T(8,128)(2,1)} %broadcast_select_fusion.1), channel_id=1, source_target_pairs={{0,2},{2,4},{4,6},{6,7},{7,5},{5,3},{3,1},{1,0},{10,8},{12,10},{14... | collective-permute-start | bytes 1228808 | tf_op jit(solution)/shard_map/ppermute | solution.py:332
  132.3 3.7 %copy-start.5 = (bf16[1,3,1024,256]{3,2,1,0:T(8,128)(2,1)S(1)}, bf16[1,3,1024,256]{3,2,1,0:T(8,128)(2,1)}, u32[]{:S(2)}) copy-start(bf16[1,3,1024,256]{3,2,1,0:T(8,128)(2,1)} %refs_0_.1) | copy-start | bytes 4718596
  135.9 10.8 %collective-permute-start.234 = (bf16[192,1024]{1,0:T(8,128)(2,1)S(1)}, bf16[192,1024]{1,0:T(8,128)(2,1)S(1)}, u32[]{:S(2)}, u32[]{:S(2)}) collective-permute-start(bf16[192,1024]{1,0:T(8,128)(2,1)S(1)} %shard_map.115), channel_id=1, source_target_pairs={{0,2},{2,4},{4,6},{6,7},{7,5},{5,3},{3,1},{1,0},{10,8},{12,10},{14... | collective-permute-start | bytes 1179656 | tf_op jit(solution)/shard_map/ppermute | solution.py:336
  142.3 4.3 %copy-start.2 = (f32[96,1024]{1,0:T(8,128)}, f32[96,1024]{1,0:T(8,128)S(1)}, u32[]{:S(2)}) copy-start(f32[96,1024]{1,0:T(8,128)S(1)} %get-tuple-element.445) | copy-start | bytes 1179652
  147.0 9.6 %collective-permute-start.241 = (bf16[96,1024]{1,0:T(8,128)(2,1)S(1)}, bf16[96,1024]{1,0:T(8,128)(2,1)S(1)}, u32[]{:S(2)}, u32[]{:S(2)}) collective-permute-start(bf16[96,1024]{1,0:T(8,128)(2,1)S(1)} %get-tuple-element.474), channel_id=1, source_target_pairs={{0,2},{2,4},{4,6},{6,7},{7,5},{5,3},{3,1},{1,0},{8,10},{10,12},{12... | collective-permute-start | bytes 589832 | tf_op jit(solution)/shard_map/ppermute | solution.py:346
  152.5 7.8 %collective-permute-start.244 = (bf16[96,1024]{1,0:T(8,128)(2,1)S(1)}, bf16[96,1024]{1,0:T(8,128)(2,1)S(1)}, u32[]{:S(2)}, u32[]{:S(2)}) collective-permute-start(bf16[96,1024]{1,0:T(8,128)(2,1)S(1)} %get-tuple-element.475), channel_id=1, source_target_pairs={{0,2},{2,4},{4,6},{6,7},{7,5},{5,3},{3,1},{1,0},{8,10},{10,12},{12... | collective-permute-start | bytes 589832 | tf_op jit(solution)/shard_map/ppermute | solution.py:346
  154.5 7.9 %collective-permute-start.235 = (bf16[96,1024]{1,0:T(8,128)(2,1)S(1)}, bf16[96,1024]{1,0:T(8,128)(2,1)S(1)}, u32[]{:S(2)}, u32[]{:S(2)}) collective-permute-start(bf16[96,1024]{1,0:T(8,128)(2,1)S(1)} %get-tuple-element.477), channel_id=1, source_target_pairs={{2,0},{4,2},{6,4},{7,6},{5,7},{3,5},{1,3},{0,1},{10,8},{12,10},{14... | collective-permute-start | bytes 589832 | tf_op jit(solution)/shard_map/ppermute | solution.py:345
  154.6 11.3 %collective-permute-start.238 = (bf16[96,1024]{1,0:T(8,128)(2,1)S(1)}, bf16[96,1024]{1,0:T(8,128)(2,1)S(1)}, u32[]{:S(2)}, u32[]{:S(2)}) collective-permute-start(bf16[96,1024]{1,0:T(8,128)(2,1)S(1)} %get-tuple-element.476), channel_id=1, source_target_pairs={{2,0},{4,2},{6,4},{7,6},{5,7},{3,5},{1,3},{0,1},{10,8},{12,10},{14... | collective-permute-start | bytes 589832 | tf_op jit(solution)/shard_map/ppermute | solution.py:345
  156.7 10.0 %collective-permute-start.242 = (bf16[96,1024]{1,0:T(8,128)(2,1)S(1)}, bf16[96,1024]{1,0:T(8,128)(2,1)S(1)}, u32[]{:S(2)}, u32[]{:S(2)}) collective-permute-start(bf16[96,1024]{1,0:T(8,128)(2,1)S(1)} %add_convert_fusion.4), channel_id=1, source_target_pairs={{0,2},{2,4},{4,6},{6,7},{7,5},{5,3},{3,1},{1,0},{8,10},{10,12},{12... | collective-permute-start | bytes 589832 | tf_op jit(solution)/shard_map/ppermute | solution.py:346
  160.4 8.7 %collective-permute-start.245 = (bf16[96,1024]{1,0:T(8,128)(2,1)S(1)}, bf16[96,1024]{1,0:T(8,128)(2,1)S(1)}, u32[]{:S(2)}, u32[]{:S(2)}) collective-permute-start(bf16[96,1024]{1,0:T(8,128)(2,1)S(1)} %add_convert_fusion.1), channel_id=1, source_target_pairs={{0,2},{2,4},{4,6},{6,7},{7,5},{5,3},{3,1},{1,0},{8,10},{10,12},{12... | collective-permute-start | bytes 589832 | tf_op jit(solution)/shard_map/ppermute | solution.py:346
  162.4 9.4 %collective-permute-start.236 = (bf16[96,1024]{1,0:T(8,128)(2,1)S(1)}, bf16[96,1024]{1,0:T(8,128)(2,1)S(1)}, u32[]{:S(2)}, u32[]{:S(2)}) collective-permute-start(bf16[96,1024]{1,0:T(8,128)(2,1)S(1)} %add_convert_fusion.10), channel_id=1, source_target_pairs={{2,0},{4,2},{6,4},{7,6},{5,7},{3,5},{1,3},{0,1},{10,8},{12,10},{14... | collective-permute-start | bytes 589832 | tf_op jit(solution)/shard_map/ppermute | solution.py:345
  166.0 7.3 %collective-permute-start.239 = (bf16[96,1024]{1,0:T(8,128)(2,1)S(1)}, bf16[96,1024]{1,0:T(8,128)(2,1)S(1)}, u32[]{:S(2)}, u32[]{:S(2)}) collective-permute-start(bf16[96,1024]{1,0:T(8,128)(2,1)S(1)} %add_convert_fusion.7), channel_id=1, source_target_pairs={{2,0},{4,2},{6,4},{7,6},{5,7},{3,5},{1,3},{0,1},{10,8},{12,10},{14... | collective-permute-start | bytes 589832 | tf_op jit(solution)/shard_map/ppermute | solution.py:345
  166.7 9.9 %copy-start = (f32[1,3,1024,256]{3,2,1,0:T(8,128)S(1)}, f32[1,3,1024,256]{3,2,1,0:T(8,128)}, u32[]{:S(2)}) copy-start(f32[1,3,1024,256]{3,2,1,0:T(8,128)} %refs_1_.3) | copy-start | bytes 9437188
  167.4 15.9 %collective-permute-start.243 = (bf16[96,1024]{1,0:T(8,128)(2,1)}, bf16[96,1024]{1,0:T(8,128)(2,1)}, u32[]{:S(2)}, u32[]{:S(2)}) collective-permute-start(bf16[96,1024]{1,0:T(8,128)(2,1)} %add_convert_fusion.3), channel_id=1, source_target_pairs={{0,2},{2,4},{4,6},{6,7},{7,5},{5,3},{3,1},{1,0},{8,10},{10,12},{12... | collective-permute-start | bytes 589832 | tf_op jit(solution)/shard_map/ppermute | solution.py:346
  169.8 13.6 %collective-permute-start.246 = (bf16[96,1024]{1,0:T(8,128)(2,1)}, bf16[96,1024]{1,0:T(8,128)(2,1)}, u32[]{:S(2)}, u32[]{:S(2)}) collective-permute-start(bf16[96,1024]{1,0:T(8,128)(2,1)} %add_convert_fusion), channel_id=1, source_target_pairs={{0,2},{2,4},{4,6},{6,7},{7,5},{5,3},{3,1},{1,0},{8,10},{10,12},{12... | collective-permute-start | bytes 589832 | tf_op jit(solution)/shard_map/ppermute | solution.py:346
  172.5 10.9 %collective-permute-start.237 = (bf16[96,1024]{1,0:T(8,128)(2,1)}, bf16[96,1024]{1,0:T(8,128)(2,1)}, u32[]{:S(2)}, u32[]{:S(2)}) collective-permute-start(bf16[96,1024]{1,0:T(8,128)(2,1)} %add_convert_fusion.9), channel_id=1, source_target_pairs={{2,0},{4,2},{6,4},{7,6},{5,7},{3,5},{1,3},{0,1},{10,8},{12,10},{14... | collective-permute-start | bytes 589832 | tf_op jit(solution)/shard_map/ppermute | solution.py:345
  174.0 9.3 %collective-permute-start.240 = (bf16[96,1024]{1,0:T(8,128)(2,1)}, bf16[96,1024]{1,0:T(8,128)(2,1)}, u32[]{:S(2)}, u32[]{:S(2)}) collective-permute-start(bf16[96,1024]{1,0:T(8,128)(2,1)} %add_convert_fusion.6), channel_id=1, source_target_pairs={{2,0},{4,2},{6,4},{7,6},{5,7},{3,5},{1,3},{0,1},{10,8},{12,10},{14... | collective-permute-start | bytes 589832 | tf_op jit(solution)/shard_map/ppermute | solution.py:345
  176.6 1.9 %copy-start.1 = (f32[1,3,1024,256]{3,2,1,0:T(8,128)S(1)}, f32[1,3,1024,256]{3,2,1,0:T(8,128)}, u32[]{:S(2)}) copy-start(f32[1,3,1024,256]{3,2,1,0:T(8,128)} %refs_2_.5) | copy-start | bytes 9437188
  178.5 4.8 %copy-start.3 = (f32[96,1024]{1,0:T(8,128)S(1)}, f32[96,1024]{1,0:T(8,128)}, u32[]{:S(2)}) copy-start(f32[96,1024]{1,0:T(8,128)} %copy-done.2) | copy-start | bytes 1179652
